TPU v7x, 32 devices: a whole 2x2x4 slice. The times are simulated.
32 devices in a mesh: groups: 2 (over y), gx: 4 (over z), gy: 4 (over x, core).
Axes of the slice: x: 2, y: 2, z: 4, core: 2. Of those that a mesh axis runs over, the one named last changes fastest.
Arguments:
- stored_rows: bfloat16 [320, 16384], P(('groups', 'gy'), 'gx'), parts along dimension 0, may hold values from -6 to 6
- new_rows: bfloat16 [16, 16384], P(('groups', 'gy'), 'gx'), parts along dimension 0, may hold values from -6 to 6
- w_query: bfloat16 [16384, 8192], P('gx', 'gy'), may hold values from -0.046875 to 0.046875
- w_key: bfloat16 [16384, 512], P('gx', 'gy'), may hold values from -0.046875 to 0.046875
- w_value: bfloat16 [16384, 512], P('gx', 'gy'), may hold values from -0.046875 to 0.046875
- w_out: bfloat16 [8192, 16384], P('gy', 'gx'), may hold values from -0.0625 to 0.0625
- kv_cache: bfloat16 [2, 16, 512, 512], P(None, ('groups', 'gx'), None, 'gy'), parts along dimension 1, may hold values from -52 to 52
- cache_len: int32 [16], P(('groups', 'gx')), parts along dimension 0, may hold values from 1 to 512, as said below
- owner: int32 [8], P('groups'), parts along dimension 0, may hold values from 0 to 3, as said below
Outputs:
- mixed: bfloat16 [16, 16384], P(('groups', 'gy'), 'gx'), parts along dimension 0
- rebuilt_key: bfloat16 [8, 40, 512], P(('groups', 'gx'), None, 'gy'), parts along dimension 0
- rebuilt_value: bfloat16 [8, 40, 512], P(('groups', 'gx'), None, 'gy'), parts along dimension 0
There are 2 independent parts, one for each index of `groups`. A program takes and returns all parts, laid end to end along the dimension named above; an argument that names none is the same for every part. Nothing has to cross between parts.
Inputs may be any that keep to these rules, and one draw needn't show every extreme that they name: A permutation: each owner index takes exactly one conversation. Only a row's first cache_len slots hold data; some row has all 512 slots in use.
All inputs are finite; a program needn't handle non-finite values.
Results may differ from a plain program's by a relative error of at most 0.013.
Values may be sent and summed in bfloat16 or wider, within the bound.
A program may use at most 64 MiB of HBM per device.

v0:
```python
import math

import jax
import jax.numpy as jnp
from jax import lax
from jax.sharding import PartitionSpec as P

HD = 128
LC = 40
ROWS_DEV = 2


BASE = 500000.0


def rotate(incoming_values, position):
    half = incoming_values.shape[-1] // 2
    index_row = jnp.arange(half).astype(jnp.float32)
    frequency = jnp.exp(index_row * (-2.0 * math.log(BASE) / incoming_values.shape[-1]))
    angle = position.astype(jnp.float32)[..., None] * frequency
    cosine = jnp.cos(angle)
    sine = jnp.sin(angle)
    first_half = incoming_values[..., :half]
    second_half = incoming_values[..., half:]
    return jnp.concatenate(
        [first_half * cosine - second_half * sine, second_half * cosine + first_half * sine],
        axis=-1,
    )


def per_device(stored_rows, new_rows, w_query, w_key, w_value, w_out, kv_cache, cache_len, owner):
    owners = lax.axis_size("gx")
    key_cols = w_key.shape[1]
    query_cols = w_query.shape[1]
    heads_here = key_cols // HD
    group_size = query_cols // key_cols
    slot_ids = jnp.arange(owners, dtype=jnp.int32)
    stored_all, fresh_all = (
        lax.all_gather(stored_rows, "gy", axis=0, tiled=True),
        lax.all_gather(new_rows, "gy", axis=0, tiled=True),
    )
    inverse = jnp.sum(jnp.where(owner[None, :] == slot_ids[:, None], slot_ids[None, :], 0), axis=1)
    source_rows = stored_all.reshape(owners, LC, stored_all.shape[1])[inverse].reshape(
        owners * LC, stored_all.shape[1]
    )
    count = 1 * lax.axis_size("gx")
    pieces = []
    pieces.append(
        jnp.dot(source_rows, w_key, preferred_element_type=jnp.float32).reshape(
            count, LC * key_cols
        )
    )
    pieces.append(
        jnp.dot(source_rows, w_value, preferred_element_type=jnp.float32).reshape(
            count, LC * key_cols
        )
    )
    pieces.append(
        jnp.dot(fresh_all, w_query, preferred_element_type=jnp.float32).reshape(
            count, ROWS_DEV * query_cols
        )
    )
    pieces.append(
        jnp.dot(fresh_all, w_key, preferred_element_type=jnp.float32).reshape(
            count, ROWS_DEV * key_cols
        )
    )
    pieces.append(
        jnp.dot(fresh_all, w_value, preferred_element_type=jnp.float32).reshape(
            count, ROWS_DEV * key_cols
        )
    )
    received = lax.psum_scatter(
        jnp.concatenate(pieces, axis=1), "gx", scatter_dimension=0, tiled=True
    )[0]
    trailing_columns = LC * key_cols
    offset = 0
    own_key = received[:trailing_columns].reshape(LC, key_cols)
    own_value = received[trailing_columns : 2 * trailing_columns].reshape(LC, key_cols)
    offset = 2 * trailing_columns
    query = received[offset : offset + ROWS_DEV * query_cols].reshape(ROWS_DEV, query_cols)
    offset = offset + ROWS_DEV * query_cols
    fresh_key = received[offset : offset + ROWS_DEV * key_cols].reshape(ROWS_DEV, key_cols)
    offset = offset + ROWS_DEV * key_cols
    fresh_value = received[offset : offset + ROWS_DEV * key_cols].reshape(ROWS_DEV, key_cols)
    first_len = cache_len[0]
    tail_pos = first_len + jnp.arange(LC, dtype=jnp.int32)
    rebuilt_key = (
        rotate(own_key.reshape(LC, heads_here, HD), tail_pos[:, None])
        .reshape(LC, key_cols)
        .astype(jnp.bfloat16)
    )
    rebuilt_value = own_value.astype(jnp.bfloat16)
    resumed = jnp.arange(ROWS_DEV, dtype=jnp.int32) == 0
    new_pos = cache_len + jnp.where(resumed, LC, 0).astype(jnp.int32)
    query_rot = rotate(query.reshape(ROWS_DEV, query_cols // HD, HD), new_pos[:, None]).astype(
        jnp.bfloat16
    )
    rotary_key_rows = rotate(fresh_key.reshape(ROWS_DEV, heads_here, HD), new_pos[:, None]).astype(
        jnp.bfloat16
    )
    value_new = fresh_value.reshape(ROWS_DEV, heads_here, HD).astype(jnp.bfloat16)
    score_scaling_factor = 1.0 / math.sqrt(HD)
    slots_cache = kv_cache.shape[2]
    grouped_query_heads = query_rot.reshape(ROWS_DEV, heads_here, group_size, HD)
    cached_keys_lookup = kv_cache[0].reshape(ROWS_DEV, slots_cache, heads_here, HD)
    cache_value = kv_cache[1].reshape(ROWS_DEV, slots_cache, heads_here, HD)
    tail_key = rebuilt_key.reshape(LC, heads_here, HD)
    tail_value = rebuilt_value.reshape(LC, heads_here, HD)
    live_row_mask = jnp.arange(slots_cache, dtype=jnp.int32)[None, :] < cache_len[:, None]
    s_cache = (
        jnp.einsum(
            "bkgd,blkd->bkgl",
            grouped_query_heads,
            cached_keys_lookup,
            preferred_element_type=jnp.float32,
        )
        * score_scaling_factor
    )
    s_cache = jnp.where(live_row_mask[:, None, None, :], s_cache, -jnp.inf)
    s_tail = (
        jnp.einsum(
            "bkgd,tkd->bkgt", grouped_query_heads, tail_key, preferred_element_type=jnp.float32
        )
        * score_scaling_factor
    )
    s_tail = jnp.where(resumed[:, None, None, None], s_tail, -jnp.inf)
    self_score = (
        jnp.einsum(
            "hzrt,hzt->hzr",
            grouped_query_heads,
            rotary_key_rows,
            preferred_element_type=jnp.float32,
        )
        * score_scaling_factor
    )
    highest = jnp.maximum(
        jnp.maximum(jnp.max(s_cache, axis=-1), jnp.max(s_tail, axis=-1)), self_score
    )
    e_cache = jnp.exp(s_cache - highest[..., None])
    e_tail = jnp.exp(s_tail - highest[..., None])
    e_self = jnp.exp(self_score - highest)
    denominator = jnp.sum(e_cache, axis=-1) + jnp.sum(e_tail, axis=-1) + e_self
    w_cache = (e_cache / denominator[..., None]).astype(jnp.bfloat16)
    w_tail = (e_tail / denominator[..., None]).astype(jnp.bfloat16)
    w_self = (e_self / denominator).astype(jnp.bfloat16)
    attn = jnp.einsum("bkgl,blkd->bkgd", w_cache, cache_value, preferred_element_type=jnp.float32)
    attn = attn + jnp.einsum(
        "bkgt,tkd->bkgd", w_tail, tail_value, preferred_element_type=jnp.float32
    )
    attn = (
        attn + w_self.astype(jnp.float32)[..., None] * value_new.astype(jnp.float32)[:, :, None, :]
    )
    attn = attn.reshape(ROWS_DEV, query_cols).astype(jnp.bfloat16)
    partial_out = jnp.dot(
        lax.all_gather(attn, "gx", axis=0, tiled=True), w_out, preferred_element_type=jnp.float32
    )
    mixed = lax.psum_scatter(
        partial_out.astype(jnp.bfloat16), "gy", scatter_dimension=0, tiled=True
    )
    return (mixed, rebuilt_key[None], rebuilt_value[None])


def solution(mesh):
    in_specs = (
        P(("groups", "gy"), "gx"),
        P(("groups", "gy"), "gx"),
        P("gx", "gy"),
        P("gx", "gy"),
        P("gx", "gy"),
        P("gy", "gx"),
        P(None, ("groups", "gx"), None, "gy"),
        P(("groups", "gx")),
        P("groups"),
    )
    out_specs = (
        P(("groups", "gy"), "gx"),
        P(("groups", "gx"), None, "gy"),
        P(("groups", "gx"), None, "gy"),
    )
    return jax.shard_map(
        per_device, mesh=mesh, in_specs=in_specs, out_specs=out_specs, check_vma=False
    )
```

profile of v0, /device:TPU:0, one launch (start us, length us, event | category | flops | bytes accessed | tf_op | source)
XLA Modules:
  0.0 145.3 jit_solution(7778349608240214939)
XLA Ops:
  7.2 0.7 all-gather.4.cloned.1.call-update
  8.0 6.5 %all-gather = bf16[4,2,4096]{2,1,0:T(2,128)(2,1)S(1)} all-gather(bf16[1,2,4096]{2,1,0:T(2,128)(2,1)} %bitcast.90), channel_id=1, replica_groups=mesh['groups'=2,'gx'=4,'gy'=4] {'gy'}, dimensions={0}, use_global_device_ids=true | all-gather | bytes 81920 | tf_op jit(solution)/shard_map/all_gather | solution.py:40
  14.4 8.5 %fusion.49 = f32[8,2048]{1,0:T(8,128)S(1)} fusion(bf16[8,4096]{1,0:T(8,128)(2,1)S(1)} %reshape.455, bf16[4096,2048]{1,0:T(8,128)(2,1)} %param.11), kind=kOutput, calls=%fused_computation.93 | convolution fusion | flops 134217728 | bytes 16908288 | tf_op jit(solution)/shard_map/dot_general | solution.py:59
  23.0 0.2 fusion.50
  23.2 0.6 reshape.440
  23.8 0.3 copy-done.1
  24.1 0.2 fusion.51
  24.4 0.6 reshape.441
  25.0 0.6 multiply_exponential_fusion
  25.6 0.5 iota_compare_fusion.2
  26.1 0.1 select_reduce_fusion
  26.2 0.5 add_convert_fusion.2
  26.8 0.6 iota_compare_fusion
  27.4 3.0 %all-gather.4.cloned.1.call-done = bf16[160,4096]{1,0:T(8,128)(2,1)} async-done(((bf16[40,4096]{1,0:T(8,128)(2,1)}), bf16[160,4096]{1,0:T(8,128)(2,1)}) %all-gather.4.cloned.1.call-update) | async-done | bytes 1310736 | tf_op jit(solution)/shard_map/all_gather | solution.py:39
  30.5 1.9 %gather_fusion = bf16[4,40,4096]{2,1,0:T(8,128)(2,1)S(1)} fusion(bf16[4,40,4096]{2,1,0:T(8,128)(2,1)} %bitcast.85, s32[1024]{0:T(1024)S(1)} %pad_clamp_fusion), kind=kCustom, calls=%fused_computation | custom fusion | bytes 2621456 | tf_op jit(solution)/shard_map/gather | solution.py:43
  32.4 1.1 fusion.47
  33.5 0.5 fusion.48
  34.1 1.0 reshape.437
  35.1 0.7 constant_dynamic-update-slice_fusion.1
  35.8 0.7 constant_dynamic-update-slice_fusion
  36.5 0.7 copy-done.2
  37.2 0.0 all-reduce.7.cloned.1.call-start
  37.3 0.7 add_convert_fusion.1
  38.0 1.2 dynamic-slice
  39.2 1.2 dynamic-slice.2
  41.1 0.8 multiply_cosine_fusion.2
  41.9 30.7 %all-reduce.5.cloned.1.call-done = f32[4,14848]{1,0:T(4,128)} async-done(((f32[4,14848]{1,0:T(4,128)}), f32[4,14848]{1,0:T(4,128)}) %all-reduce.5.cloned.1.call-update) | async-done | bytes 237584
  72.6 1.4 dynamic-slice.6
  74.0 0.8 fusion.42
  74.8 0.1 maximum_bitcast_fusion.3
  74.9 1.6 %constant_dynamic-slice_fusion = f32[1,5120]{1,0:T(1,128)S(1)} fusion(f32[4,14848]{1,0:T(4,128)} %all-reduce.5.cloned.1.call-done, u32[]{:T(128)} %bitcast.27), kind=kLoop, calls=%fused_computation.79 | loop fusion | bytes 40964 | tf_op jit(solution)/shard_map/slice | solution.py:78
  76.4 0.8 fusion.19
  77.3 1.6 %dynamic-slice.4 = f32[1,4096]{1,0:T(1,128)S(1)} dynamic-slice(f32[4,14848]{1,0:T(4,128)} %all-reduce.5.cloned.1.call-done, u32[]{:T(128)} %bitcast.27, u32[]{:T(128)S(6)} %convert.36), dynamic_slice_sizes={1,4096} | dynamic-slice | bytes 32772 | tf_op jit(solution)/shard_map/slice | solution.py:81
  78.9 0.1 subtract_convert_fusion
  79.0 0.2 fusion.36
  79.2 0.3 fusion.45
  79.5 0.3 fusion.46
  79.8 0.2 fusion.23
  79.9 0.2 fusion.11
  80.1 0.2 convolution_bitcast_fusion.1
  80.4 1.7 %fusion.22 = bf16[5120]{0:T(1024)(128)(2,1)S(1)} fusion(f32[4,14848]{1,0:T(4,128)} %all-reduce.5.cloned.1.call-done, u32[]{:T(128)} %bitcast.27, u32[]{:T(128)S(6)} %convert.38), kind=kLoop, calls=%fused_computation.33 | loop fusion | bytes 20488 | tf_op jit(solution)/shard_map/convert_element_type | solution.py:93
  82.1 1.4 fusion.35
  83.5 0.2 fusion.4
  83.7 13.1 %all-gather.1 = bf16[4,2,2048]{2,1,0:T(2,128)(2,1)S(1)} all-gather(bf16[1,2,2048]{2,1,0:T(2,128)(2,1)S(1)} %reshape.456), channel_id=1, replica_groups=mesh['groups'=2,'gx'=4,'gy'=4] {'gx'}, dimensions={0}, use_global_device_ids=true | all-gather | bytes 40960 | tf_op jit(solution)/shard_map/all_gather | solution.py:156
  96.8 8.7 %convolution_convert_fusion = bf16[8,4096]{1,0:T(8,128)(2,1)} fusion(bf16[8,2048]{1,0:T(8,128)(2,1)S(1)} %reshape.457, bf16[2048,4096]{1,0:T(8,128)(2,1)} %param.14), kind=kOutput, calls=%fused_computation.1 | convolution fusion | flops 134250496 | bytes 16875520 | tf_op jit(solution)/shard_map/dot_general | solution.py:155
  105.5 0.7 maximum_bitcast_fusion.2
  106.2 31.2 %all-reduce.7.cloned.1.call-done = bf16[8,4096]{1,0:T(8,128)(2,1)} async-done(((bf16[8,4096]{1,0:T(8,128)(2,1)}), bf16[8,4096]{1,0:T(8,128)(2,1)}) %all-reduce.7.cloned.1.call-update) | async-done | bytes 65552
  137.3 1.5 %constant_dynamic-slice_fusion.1 = bf16[2,4096]{1,0:T(2,128)(2,1)} fusion(bf16[8,4096]{1,0:T(8,128)(2,1)} %all-reduce.7.cloned.1.call-done, u32[]{:T(128)S(6)} %multiply.3), kind=kLoop, calls=%fused_computation.80 | loop fusion | bytes 32772
  (32 shorter events, 0.4 us)
Async XLA Ops:
  7.2 15.8 %copy-start = (bf16[4096,128]{1,0:T(8,128)(2,1)S(1)}, bf16[4096,128]{1,0:T(8,128)(2,1)}, u32[]{:S(2)}) copy-start(bf16[4096,128]{1,0:T(8,128)(2,1)} %param.12) | copy-start | bytes 3145732
  7.2 23.3 %all-gather.4.cloned.1.call-start = ((), (), s32[]{:S(2)}) async-start(), calls=%async_computation | async-start | bytes 1638400 | tf_op jit(solution)/shard_map/all_gather | solution.py:39
  7.9 64.7 %all-reduce.5.cloned.1.call-start = ((), (), s32[]{:S(2)}) async-start(), calls=%async_computation.1 | async-start | bytes 475136
  22.9 1.2 copy-start.1
  22.9 3.2 %copy-start.8 = (s32[4]{0:T(128)S(1)}, s32[4]{0:T(128)}, u32[]{:S(2)}) copy-start(s32[4]{0:T(128)} %param.17) | copy-start | bytes 52
  22.9 3.3 %copy-start.7 = (s32[2]{0:T(128)S(1)}, s32[2]{0:T(128)}, u32[]{:S(2)}) copy-start(s32[2]{0:T(128)} %param.16) | copy-start | bytes 28
  34.0 45.1 %copy-start.3 = (bf16[2,2,512,128]{3,2,1,0:T(8,128)(2,1)S(1)}, bf16[2,2,512,128]{3,2,1,0:T(8,128)(2,1)}, u32[]{:S(2)}) copy-start(bf16[2,2,512,128]{3,2,1,0:T(8,128)(2,1)} %param.15) | copy-start | bytes 1572868
  34.0 45.1 %copy-start.5 = (pred[2,512]{1,0:T(4,128)(4,1)S(1)}, pred[2,512]{1,0:T(4,128)(4,1)}, u32[]{:S(2)}) copy-start(pred[2,512]{1,0:T(4,128)(4,1)} %iota_compare_fusion) | copy-start | bytes 3076
  34.1 45.4 %copy-start.6 = (pred[2]{0:T(512)(128)(4,1)S(1)}, pred[2]{0:T(512)(128)(4,1)}, u32[]{:S(2)}) copy-start(pred[2]{0:T(512)(128)(4,1)} %iota_compare_fusion.2) | copy-start | bytes 10
  36.5 0.7 copy-start.2
  37.2 100.1 %all-reduce.7.cloned.1.call-start = ((), (), s32[]{:S(2)}) async-start(), calls=%async_computation.2 | async-start | bytes 131072
  82.1 23.4 %copy-start.4 = (bf16[5120]{0:T(1024)(128)(2,1)}, bf16[5120]{0:T(1024)(128)(2,1)S(1)}, u32[]{:S(2)}) copy-start(bf16[5120]{0:T(1024)(128)(2,1)S(1)} %fusion.22) | copy-start | bytes 30724
Sparse Core Ops, SparseCore 0:
  9.5 20.8 all-gather.3
  37.4 35.1 all-reduce.4
  105.6 31.6 all-reduce.6
where the time goes:
time: 146 us; the launch traced here: 145 us
  waiting for transfers between devices  65.7 us (45%)
  matrix products  20.4 us (14%)
  blocking collectives  19.5 us (13%)
  local copies, waits for them, and re-layouts  17 us (12%)
  between operations  14.6 us (10%)
  other arithmetic  8.05 us (6%)
    unnamed x5, waiting for transfers between devices  62.6 us
    all_gather x1, blocking collectives, per_device(): lax.all_gather(attn, 'gx', axis=0, tiled=True)  13.1 us
    dot_general x1, matrix products, per_device(): jnp.dot(lax.all_gather(attn, 'gx', axis=0, tiled=True), w_out, preferred_...  8.66 us
    dot_general x1, matrix products, per_device(): jnp.dot(fresh_all, w_query, preferred_element_type=jnp.float32)  8.45 us
    all_gather x1, blocking collectives, per_device(): lax.all_gather(new_rows, 'gy', axis=0, tiled=True)  6.46 us
    unnamed x28, local copies, waits for them, and re-layouts  5.79 us
    all_gather x1, waiting for transfers between devices, per_device(): lax.all_gather(stored_rows, 'gy', axis=0, tiled=True)  3.03 us
  transfers between devices with their start and end apart: 3, of which 3 were waited for; matrix products, arithmetic and copies ran while one was open for 12% of the time, Pallas kernels for 0%

commit v1 on v0

v1 whole, which is shorter than its diff:
```python
import functools
import math

import jax
import jax.numpy as jnp
from jax import lax
from jax.experimental import pallas as pl
from jax.experimental.pallas import tpu as pltpu
from jax.sharding import PartitionSpec as P

HD = 128
LC = 40
TAIL = 48
PAD = 128
ROWS_DEV = 2
BASE = 500000.0
F32 = jnp.float32
BF16 = jnp.bfloat16
MESH = pl.DeviceIdType.MESH


def rope_tables(first_position, rows):
    lane = lax.broadcasted_iota(jnp.int32, (rows, HD), 1)
    row = lax.broadcasted_iota(jnp.int32, (rows, HD), 0)
    index = jnp.where(lane < HD // 2, lane, lane - HD // 2).astype(F32)
    frequency = jnp.exp(index * (-2.0 * math.log(BASE) / HD))
    angle = (row + first_position).astype(F32) * frequency
    sine = jnp.sin(angle)
    return jnp.cos(angle), jnp.where(lane < HD // 2, -sine, sine)


def rope(values, cosine, sine):
    return values * cosine + pltpu.roll(values, HD // 2, 1) * sine


def dot(a, b):
    return jnp.dot(a, b, preferred_element_type=F32)


def layer_kernel(
    nx, ny,
    len_ref, owner_ref, stored_ref, new_ref, wq_ref, wk_ref, wv_ref, wo_ref, kv_ref,
    mixed_ref, rkey_ref, rvalue_ref,
    wq, wkv, wo, stored, new, lhs, kv, q_acc, q_out, q_in, part, kv_out, kv_in,
    attn_all, o_out, o_in,
    wq_sem, wkv_sem, wo_sem, kv_sem, own_sem, new_local_sem,
    new_send, new_recv, st_send, st_recv, q_send, q_recv, kvp_send, kvp_recv,
    at_send, at_recv, o_send, o_recv,
):
    x = lax.axis_index("gx")
    y = lax.axis_index("gy")
    features = wq_ref.shape[0]
    qcols = wq_ref.shape[1]
    kcols = wk_ref.shape[1]
    heads = qcols // HD
    slots = kv_ref.shape[2]
    nq = wq_sem.shape[0]
    kc = features // nq
    wo_rows = wo_ref.shape[0] // nq
    nst = own_sem.shape[0]
    fc = features // nst
    conv_here = stored_ref.shape[0] // LC
    rows_here = new_ref.shape[0]
    rows = rows_here * ny
    width = wo_ref.shape[1]
    halves = o_send.shape[1]

    def wq_copy(i):
        r = pl.ds(pl.multiple_of(i * kc, kc), kc)
        return pltpu.make_async_copy(wq_ref.at[r, :], wq.at[r, :], wq_sem.at[i])

    def wo_copy(i):
        r = pl.ds(pl.multiple_of(i * wo_rows, wo_rows), wo_rows)
        return pltpu.make_async_copy(wo_ref.at[r, :], wo.at[r, :], wo_sem.at[i])

    def st_own(j):
        return pltpu.make_async_copy(
            stored_ref.at[:, pl.ds(j * fc, fc)], stored.at[y, :, pl.ds(j * fc, fc)], own_sem.at[j]
        )

    wk_copy = pltpu.make_async_copy(wk_ref, wkv.at[:, pl.ds(0, kcols)], wkv_sem.at[0])
    wv_copy = pltpu.make_async_copy(wv_ref, wkv.at[:, pl.ds(kcols, kcols)], wkv_sem.at[1])
    new_own = pltpu.make_async_copy(new_ref, new.at[y], new_local_sem.at[0])
    kv_copy = pltpu.make_async_copy(kv_ref, kv.at[:, :, pl.ds(0, slots), :], kv_sem.at[0])

    new_own.start()
    for i in range(nq):
        wq_copy(i).start()
    wk_copy.start()
    wv_copy.start()
    for j in range(nst):
        st_own(j).start()
    kv_copy.start()

    barrier = pltpu.get_barrier_semaphore()
    for d in range(1, nx):
        pl.semaphore_signal(
            barrier, inc=1, device_id={"gx": lax.rem(x + d, nx)}, device_id_type=MESH
        )
    for d in range(1, ny):
        pl.semaphore_signal(
            barrier, inc=1, device_id={"gy": lax.rem(y + d, ny)}, device_id_type=MESH
        )
    pl.semaphore_wait(barrier, nx + ny - 2)

    pair = y + 1 - 2 * lax.rem(y, 2)
    cross = lax.rem(y + 2, ny)
    far = 3 - y

    def over_gy(src, dst, ssem, rsem, target):
        return pltpu.make_async_remote_copy(
            src_ref=src, dst_ref=dst, send_sem=ssem, recv_sem=rsem,
            device_id={"gy": target}, device_id_type=MESH,
        )

    def over_gx(src, dst, ssem, rsem, target):
        return pltpu.make_async_remote_copy(
            src_ref=src, dst_ref=dst, send_sem=ssem, recv_sem=rsem,
            device_id={"gx": target}, device_id_type=MESH,
        )

    new_copies = [
        over_gy(new_ref, new.at[y], new_send.at[d], new_recv.at[d], lax.rem(y + d, ny))
        for d in range(1, ny)
    ]
    for c in new_copies:
        c.start()

    def st_copy(kind, j):
        cols = pl.ds(j * fc, fc)
        if kind == 2:
            return over_gy(
                stored.at[cross, :, cols], stored.at[cross, :, cols],
                st_send.at[2, j], st_recv.at[2, j], pair,
            )
        return over_gy(
            stored_ref.at[:, cols], stored.at[y, :, cols],
            st_send.at[kind, j], st_recv.at[kind, j], cross if kind == 1 else pair,
        )

    for kind in (1, 0):
        for j in range(nst):
            st_copy(kind, j).start()

    first_len = len_ref[0]
    cos0, sin0 = rope_tables(first_len, TAIL)
    cos1, sin1 = rope_tables(len_ref[1], 8)
    zeros = jnp.zeros((PAD - TAIL, kcols), BF16)
    for which in range(2):
        for b in range(ROWS_DEV):
            kv[which, b, pl.ds(slots + TAIL, PAD - TAIL), :] = zeros
    q_acc[...] = jnp.zeros_like(q_acc)

    new_own.wait()
    for c in new_copies:
        c.wait_recv()
    lhs[...] = jnp.concatenate([new[s].astype(F32) for s in range(ny)], axis=0).astype(BF16)

    def q_step(i, carry):
        wq_copy(i).wait()
        wo_copy(i).start()
        k = pl.ds(pl.multiple_of(i * kc, kc), kc)
        q_acc[...] += dot(lhs[:, k], wq[k, :])
        return carry

    lax.fori_loop(0, nq, q_step, 0)
    wk_copy.wait()
    wv_copy.wait()
    fresh = dot(lhs[...], wkv[...])
    for o in range(nx):
        r = slice(o * ROWS_DEV, (o + 1) * ROWS_DEV)
        q_out[o, :, pl.ds(0, qcols)] = q_acc[r, :]
        q_out[o, :, pl.ds(qcols, 2 * kcols)] = fresh[r, :]
    q_copies = []
    for d in range(1, nx):
        t = lax.rem(x + d, nx)
        c = over_gx(q_out.at[t], q_in.at[x], q_send.at[d], q_recv.at[d], t)
        c.start()
        q_copies.append(c)

    def project(source, arrive):
        total = None
        for j in range(nst):
            arrive(j)
            cols = pl.ds(j * fc, fc)
            piece = dot(stored[source, :, cols], wkv[cols, :])
            total = piece if total is None else total + piece
        for c in range(conv_here):
            part[source * conv_here + c] = total[c * LC : (c + 1) * LC, :]

    def arrive_cross(j):
        st_copy(1, j).wait_recv()
        st_copy(2, j).start()

    project(y, lambda j: st_own(j).wait())
    project(pair, lambda j: st_copy(0, j).wait_recv())
    project(cross, arrive_cross)
    project(far, lambda j: st_copy(2, j).wait_recv())

    def conversation_of(o):
        def step(c, found):
            return jnp.where(owner_ref[c] == o, c, found)
        return lax.fori_loop(0, nx, step, jnp.int32(0), unroll=nx <= 8)

    for o in range(nx):
        kv_out[o] = part[conversation_of(o)].astype(BF16)
    kvp_copies = []
    for d in range(1, nx):
        t = lax.rem(x + d, nx)
        c = over_gx(kv_out.at[t], kv_in.at[x], kvp_send.at[d], kvp_recv.at[d], t)
        c.start()
        kvp_copies.append(c)

    q_sum = q_out[x]
    for d in range(1, nx):
        q_copies[d - 1].wait_recv()
        q_sum = q_sum + q_in[lax.rem(x + nx - d, nx)]
    scale = 1.0 / math.sqrt(HD)
    at = lax.broadcasted_iota(jnp.int32, (1, slots + PAD), 1)
    tail_row = lax.broadcasted_iota(jnp.int32, (TAIL, kcols), 0)
    kv_copy.wait()

    def query_of(b, cosine, sine):
        stacked = jnp.concatenate(
            [q_sum[b : b + 1, h * HD : (h + 1) * HD] for h in range(heads)], axis=0
        )
        return rope(stacked, cosine, sine).astype(BF16)

    def attend(b, query, live):
        s = lax.dot_general(
            query, kv[0, b], (((1,), (1,)), ((), ())), preferred_element_type=F32
        ) * scale
        s = jnp.where(live, s, -jnp.inf)
        e = jnp.exp(s - jnp.max(s, axis=1, keepdims=True))
        w = (e / jnp.sum(e, axis=1, keepdims=True)).astype(BF16)
        return dot(w, kv[1, b])

    key1 = rope(q_sum[1:2, qcols : qcols + kcols], cos1[0:1], sin1[0:1])
    value1 = q_sum[1:2, qcols + kcols :]
    tail = pl.ds(slots, TAIL)
    kv[0, 1, tail, :] = jnp.where(tail_row == LC, key1, 0.0).astype(BF16)
    kv[1, 1, tail, :] = jnp.where(tail_row == LC, value1, 0.0).astype(BF16)
    attn1 = attend(1, query_of(1, cos1[0:1], sin1[0:1]), (at < len_ref[1]) | (at == slots + LC))
    query0 = query_of(0, cos0[LC : LC + 1], sin0[LC : LC + 1])

    kv_sum = part[conversation_of(x)]
    for d in range(1, nx):
        kvp_copies[d - 1].wait_recv()
        kv_sum = kv_sum + kv_in[lax.rem(x + nx - d, nx)].astype(F32)
    rest = jnp.zeros((TAIL - LC - 1, kcols), F32)
    key0 = jnp.concatenate([kv_sum[:, :kcols], q_sum[0:1, qcols : qcols + kcols], rest], axis=0)
    value0 = jnp.concatenate([kv_sum[:, kcols:], q_sum[0:1, qcols + kcols :], rest], axis=0)
    key0 = rope(key0, cos0, sin0).astype(BF16)
    value0 = value0.astype(BF16)
    kv[0, 0, tail, :] = key0
    kv[1, 0, tail, :] = value0
    rkey_ref[0] = key0[:LC]
    rvalue_ref[0] = value0[:LC]
    attn0 = attend(0, query0, (at < first_len) | ((at >= slots) & (at <= slots + LC)))

    attn_all[x] = jnp.concatenate(
        [
            jnp.concatenate([a[h : h + 1, :] for h in range(heads)], axis=1)
            for a in (attn0, attn1)
        ],
        axis=0,
    ).astype(BF16)
    at_copies = []
    for d in range(1, nx):
        c = over_gx(
            attn_all.at[x], attn_all.at[x], at_send.at[d], at_recv.at[d], lax.rem(x + d, nx)
        )
        c.start()
        at_copies.append(c)
    for i in range(nq):
        wo_copy(i).wait()
    for c in at_copies:
        c.wait_recv()
    attn = jnp.concatenate([attn_all[s].astype(F32) for s in range(nx)], axis=0).astype(BF16)

    half = width // halves
    cw = min(512, half)
    o_copies = []
    for h in range(halves):
        def o_step(i, carry):
            cols = pl.ds(pl.multiple_of(h * half + i * cw, cw), cw)
            piece = dot(attn, wo[:, cols])
            for g in range(ny):
                o_out[g, :, cols] = piece[g * rows_here : (g + 1) * rows_here].astype(BF16)
            return carry

        lax.fori_loop(0, half // cw, o_step, 0)
        cols = pl.ds(h * half, half)
        for d in range(1, ny):
            t = lax.rem(y + d, ny)
            c = over_gy(
                o_out.at[t, :, cols], o_in.at[y, :, cols], o_send.at[d, h], o_recv.at[d, h], t
            )
            c.start()
            o_copies.append(c)
    for h in range(halves):
        cols = pl.ds(h * half, half)
        total = o_out[y, :, cols].astype(F32)
        for d in range(1, ny):
            o_copies[h * (ny - 1) + d - 1].wait_recv()
            total = total + o_in[lax.rem(y + ny - d, ny), :, cols].astype(F32)
        mixed_ref[:, cols] = total.astype(BF16)

    for c in new_copies + q_copies + kvp_copies + at_copies + o_copies:
        c.wait_send()
    for kind in range(3):
        for j in range(nst):
            st_copy(kind, j).wait_send()


def per_device(stored_rows, new_rows, w_query, w_key, w_value, w_out, kv_cache, cache_len, owner):
    nx, ny = lax.axis_size("gx"), lax.axis_size("gy")
    features, qcols = w_query.shape
    kcols = w_key.shape[1]
    width = w_out.shape[1]
    slots = kv_cache.shape[2]
    rows_here = new_rows.shape[0]
    rows = rows_here * ny
    nq = max(1, features // 512)
    nst = max(1, features // 1024)
    halves = 2 if width >= 1024 else 1
    dma = pltpu.SemaphoreType.DMA
    hbm = pl.BlockSpec(memory_space=pl.ANY)
    smem = pl.BlockSpec(memory_space=pltpu.SMEM)
    vmem = pl.BlockSpec(memory_space=pltpu.VMEM)
    return pl.pallas_call(
        functools.partial(layer_kernel, nx, ny),
        out_shape=(
            jax.ShapeDtypeStruct((rows_here, width), BF16),
            jax.ShapeDtypeStruct((1, LC, kcols), BF16),
            jax.ShapeDtypeStruct((1, LC, kcols), BF16),
        ),
        in_specs=[smem, smem] + [hbm] * 7,
        out_specs=(vmem, vmem, vmem),
        scratch_shapes=[
            pltpu.VMEM(w_query.shape, BF16),
            pltpu.VMEM((features, 2 * kcols), BF16),
            pltpu.VMEM(w_out.shape, BF16),
            pltpu.VMEM((ny,) + stored_rows.shape, BF16),
            pltpu.VMEM((ny,) + new_rows.shape, BF16),
            pltpu.VMEM((rows, features), BF16),
            pltpu.VMEM((2, ROWS_DEV, slots + PAD, kcols), BF16),
            pltpu.VMEM((rows, qcols), F32),
            pltpu.VMEM((nx, ROWS_DEV, qcols + 2 * kcols), F32),
            pltpu.VMEM((nx, ROWS_DEV, qcols + 2 * kcols), F32),
            pltpu.VMEM((nx, LC, 2 * kcols), F32),
            pltpu.VMEM((nx, LC, 2 * kcols), BF16),
            pltpu.VMEM((nx, LC, 2 * kcols), BF16),
            pltpu.VMEM((nx, ROWS_DEV, qcols), BF16),
            pltpu.VMEM((ny, rows_here, width), BF16),
            pltpu.VMEM((ny, rows_here, width), BF16),
            dma((nq,)), dma((2,)), dma((nq,)), dma((1,)), dma((nst,)), dma((1,)),
            dma((ny,)), dma((ny,)), dma((3, nst)), dma((3, nst)),
            dma((nx,)), dma((nx,)), dma((nx,)), dma((nx,)),
            dma((nx,)), dma((nx,)), dma((ny, halves)), dma((ny, halves)),
        ],
        compiler_params=pltpu.CompilerParams(
            collective_id=0, has_side_effects=True, vmem_limit_bytes=60 * 1024 * 1024
        ),
    )(cache_len, owner, stored_rows, new_rows, w_query, w_key, w_value, w_out, kv_cache)


def solution(mesh):
    in_specs = (
        P(("groups", "gy"), "gx"),
        P(("groups", "gy"), "gx"),
        P("gx", "gy"),
        P("gx", "gy"),
        P("gx", "gy"),
        P("gy", "gx"),
        P(None, ("groups", "gx"), None, "gy"),
        P(("groups", "gx")),
        P("groups"),
    )
    out_specs = (
        P(("groups", "gy"), "gx"),
        P(("groups", "gx"), None, "gy"),
        P(("groups", "gx"), None, "gy"),
    )
    return jax.shard_map(
        per_device, mesh=mesh, in_specs=in_specs, out_specs=out_specs, check_vma=False
    )
```

time: 146 us -> 37.2 us (0.25)
  waiting for transfers between devices: 65.7 us -> 0 us
  Pallas kernels: 0 us -> 32.2 us
  matrix products: 20.4 us -> 0 us
  blocking collectives: 19.5 us -> 0 us
  between operations: 14.6 us -> 0.64 us
  local copies, waits for them, and re-layouts: 17 us -> 3.94 us
  other arithmetic: 8.05 us -> 0 us
    unnamed x5 -> x0, waiting for transfers between devices: 62.6 us -> none
    pallas_call x0 -> x1, Pallas kernels: none -> 32.2 us  [per_device(): pl.pallas_call(functools.partial(layer_kernel, nx, ny), out_shape=(jax.Sh...]
    dot_general x11 -> x0, matrix products: 20.4 us -> none  [the longest x1 8.66 us: per_device(): jnp.dot(lax.all_gather(attn, 'gx', axis=0, tiled=True), w_out, preferred_...]
    all_gather x2 -> x0, blocking collectives: 19.5 us -> none  [the longest x1 13.1 us: per_device(): lax.all_gather(attn, 'gx', axis=0, tiled=True)]
    slice x3 -> x0, local copies, waits for them, and re-layouts: 4.6 us -> none  [the longest x1 1.63 us: per_device(): received[offset:offset + ROWS_DEV * query_cols]]
    convert_element_type x5 -> x0, other arithmetic: 3.29 us -> none  [the longest x1 1.4 us: per_device(): value_new.astype(jnp.float32)[:, :, None, :]]
    all_gather x1 -> x0, waiting for transfers between devices: 3.03 us -> none  [per_device(): lax.all_gather(stored_rows, 'gy', axis=0, tiled=True)]
    reshape x5 -> x0, local copies, waits for them, and re-layouts: 2.26 us -> none  [the longest x1 0.97 us: per_device(): jnp.dot(source_rows, w_key, preferred_element_type=jnp.float32)]
  transfers between devices with their start and end apart: 3 -> 0, of which waited for: 3 -> 0; matrix products, arithmetic and copies ran while one was open for 12% -> 0% of each run, Pallas kernels for 0% -> 0%
where the time goes in v1:
time: 37.2 us; the launch traced here: 36.8 us
  Pallas kernels  32.2 us (87%)
  local copies, waits for them, and re-layouts  3.94 us (11%)
  between operations  0.64 us (2%)
    pallas_call x1, Pallas kernels, per_device(): pl.pallas_call(functools.partial(layer_kernel, nx, ny), out_shape=(jax.Sh...  32.2 us
    unnamed x3, local copies, waits for them, and re-layouts  3.94 us

profile of v1, /device:TPU:0, one launch (start us, length us, event | category | flops | bytes accessed | tf_op | source)
XLA Modules:
  0.0 36.8 jit_solution(9944714723588259337)
XLA Ops:
  0.6 32.2 %shard_map.112 = (bf16[2,4096]{1,0:T(2,128)(2,1)}, bf16[1,40,128]{2,1,0:T(8,128)(2,1)}, bf16[1,40,128]{2,1,0:T(8,128)(2,1)}) custom-call(s32[2]{0:T(128)} %len_ref.1, s32[4]{0:T(128)} %owner_ref.1, bf16[40,4096]{1,0:T(8,128)(2,1)} %stored_ref.1, bf16[2,4096]{1,0:T(2,128)(2,1)} %new_ref.1, bf16[4096,2048]{1,0:T(8,128)(2,1)} %wq_ref.1, ...), custom_call_target="tpu_custom_call" | custom-call | tf_op jit(solution)/shard_map/pallas_call | solution.py:331
  32.9 1.3 %copy.15 = bf16[2,4096]{1,0:T(2,128)(2,1)} copy(bf16[2,4096]{1,0:T(2,128)(2,1)} %get-tuple-element.6) | data formatting | bytes 32768
  34.2 1.3 %copy.16 = bf16[1,40,128]{2,1,0:T(8,128)(2,1)} copy(bf16[1,40,128]{2,1,0:T(8,128)(2,1)} %get-tuple-element.7) | data formatting | bytes 20480
  35.5 1.3 %copy.17 = bf16[1,40,128]{2,1,0:T(8,128)(2,1)} copy(bf16[1,40,128]{2,1,0:T(8,128)(2,1)} %get-tuple-element.8) | data formatting | bytes 20480

commit v2 on v1

--- a/solution.py
+++ b/solution.py
@@ -147,8 +147,7 @@
     cos1, sin1 = rope_tables(len_ref[1], 8)
     zeros = jnp.zeros((PAD - TAIL, kcols), BF16)
     for which in range(2):
-        for b in range(ROWS_DEV):
-            kv[which, b, pl.ds(slots + TAIL, PAD - TAIL), :] = zeros
+        kv[which, 1, pl.ds(slots + TAIL, PAD - TAIL), :] = zeros
     q_acc[...] = jnp.zeros_like(q_acc)
 
     new_own.wait()
@@ -226,11 +225,13 @@
         )
         return rope(stacked, cosine, sine).astype(BF16)
 
+    def scores(query, keys):
+        return lax.dot_general(
+            query, keys, (((1,), (1,)), ((), ())), preferred_element_type=F32
+        ) * scale
+
     def attend(b, query, live):
-        s = lax.dot_general(
-            query, kv[0, b], (((1,), (1,)), ((), ())), preferred_element_type=F32
-        ) * scale
-        s = jnp.where(live, s, -jnp.inf)
+        s = jnp.where(live, scores(query, kv[0, b]), -jnp.inf)
         e = jnp.exp(s - jnp.max(s, axis=1, keepdims=True))
         w = (e / jnp.sum(e, axis=1, keepdims=True)).astype(BF16)
         return dot(w, kv[1, b])
@@ -242,6 +243,8 @@
     kv[1, 1, tail, :] = jnp.where(tail_row == LC, value1, 0.0).astype(BF16)
     attn1 = attend(1, query_of(1, cos1[0:1], sin1[0:1]), (at < len_ref[1]) | (at == slots + LC))
     query0 = query_of(0, cos0[LC : LC + 1], sin0[LC : LC + 1])
+    cached0 = jnp.where(at[:, :slots] < first_len, scores(query0, kv[0, 0, :slots]), -jnp.inf)
+    cached_top = jnp.max(cached0, axis=1, keepdims=True)
 
     kv_sum = part[conversation_of(x)]
     for d in range(1, nx):
@@ -252,11 +255,15 @@
     value0 = jnp.concatenate([kv_sum[:, kcols:], q_sum[0:1, qcols + kcols :], rest], axis=0)
     key0 = rope(key0, cos0, sin0).astype(BF16)
     value0 = value0.astype(BF16)
-    kv[0, 0, tail, :] = key0
-    kv[1, 0, tail, :] = value0
-    rkey_ref[0] = key0[:LC]
-    rvalue_ref[0] = value0[:LC]
-    attn0 = attend(0, query0, (at < first_len) | ((at >= slots) & (at <= slots + LC)))
+    tail0 = jnp.where(
+        lax.broadcasted_iota(jnp.int32, (1, TAIL), 1) <= LC, scores(query0, key0), -jnp.inf
+    )
+    top = jnp.maximum(cached_top, jnp.max(tail0, axis=1, keepdims=True))
+    e_cached = jnp.exp(cached0 - top)
+    e_tail = jnp.exp(tail0 - top)
+    total = jnp.sum(e_cached, axis=1, keepdims=True) + jnp.sum(e_tail, axis=1, keepdims=True)
+    attn0 = dot((e_cached / total).astype(BF16), kv[1, 0, :slots])
+    attn0 = attn0 + dot((e_tail / total).astype(BF16), value0)
 
     attn_all[x] = jnp.concatenate(
         [
@@ -272,6 +279,8 @@
         )
         c.start()
         at_copies.append(c)
+    rkey_ref[0] = key0[:LC]
+    rvalue_ref[0] = value0[:LC]
     for i in range(nq):
         wo_copy(i).wait()
     for c in at_copies:
@@ -313,6 +322,20 @@
             st_copy(kind, j).wait_send()
 
 
+def hand_over(*refs):
+    sources, results, held = refs[:3], refs[3:6], refs[6:9]
+    arrive, leave = refs[9:]
+    taken = [pltpu.make_async_copy(sources[i], held[i], arrive.at[i]) for i in range(3)]
+    given = [pltpu.make_async_copy(held[i], results[i], leave.at[i]) for i in range(3)]
+    for c in taken:
+        c.start()
+    for t, g in zip(taken, given):
+        t.wait()
+        g.start()
+    for g in given:
+        g.wait()
+
+
 def per_device(stored_rows, new_rows, w_query, w_key, w_value, w_out, kv_cache, cache_len, owner):
     nx, ny = lax.axis_size("gx"), lax.axis_size("gy")
     features, qcols = w_query.shape
@@ -323,18 +346,19 @@
     rows = rows_here * ny
     nq = max(1, features // 512)
     nst = max(1, features // 1024)
-    halves = 2 if width >= 1024 else 1
+    halves = max(1, width // 2048)
     dma = pltpu.SemaphoreType.DMA
-    hbm = pl.BlockSpec(memory_space=pl.ANY)
+    hbm = pl.BlockSpec(memory_space=pltpu.HBM)
     smem = pl.BlockSpec(memory_space=pltpu.SMEM)
     vmem = pl.BlockSpec(memory_space=pltpu.VMEM)
-    return pl.pallas_call(
+    out_shape = (
+        jax.ShapeDtypeStruct((rows_here, width), BF16),
+        jax.ShapeDtypeStruct((1, LC, kcols), BF16),
+        jax.ShapeDtypeStruct((1, LC, kcols), BF16),
+    )
+    results = pl.pallas_call(
         functools.partial(layer_kernel, nx, ny),
-        out_shape=(
-            jax.ShapeDtypeStruct((rows_here, width), BF16),
-            jax.ShapeDtypeStruct((1, LC, kcols), BF16),
-            jax.ShapeDtypeStruct((1, LC, kcols), BF16),
-        ),
+        out_shape=out_shape,
         in_specs=[smem, smem] + [hbm] * 7,
         out_specs=(vmem, vmem, vmem),
         scratch_shapes=[
@@ -363,6 +387,13 @@
             collective_id=0, has_side_effects=True, vmem_limit_bytes=60 * 1024 * 1024
         ),
     )(cache_len, owner, stored_rows, new_rows, w_query, w_key, w_value, w_out, kv_cache)
+    return pl.pallas_call(
+        hand_over,
+        out_shape=out_shape,
+        in_specs=[hbm] * 3,
+        out_specs=(hbm,) * 3,
+        scratch_shapes=[pltpu.VMEM(o.shape, o.dtype) for o in out_shape] + [dma((3,)), dma((3,))],
+    )(*results)
 
 
 def solution(mesh):

time: 37.2 us -> 34.5 us (0.927)
  local copies, waits for them, and re-layouts: 3.94 us -> 0 us
  Pallas kernels: 32.2 us -> 33.6 us
    unnamed x3 -> x0, local copies, waits for them, and re-layouts: 3.94 us -> none
    pallas_call x1 -> x2, Pallas kernels: 32.2 us -> 33.6 us  [the longest x1 32.2 us: per_device(): pl.pallas_call(functools.partial(layer_kernel, nx, ny), out_shape=out_sha...]
where the time goes in v2:
time: 34.5 us; the launch traced here: 34.2 us
  Pallas kernels  33.6 us (97%)
  between operations  0.64 us (2%)
    pallas_call x1, Pallas kernels, per_device(): pl.pallas_call(functools.partial(layer_kernel, nx, ny), out_shape=out_sha...  32.2 us
    pallas_call x1, Pallas kernels, per_device(): pl.pallas_call(hand_over, out_shape=out_shape, in_specs=[hbm] * 3, out_sp...  1.39 us

profile of v2, /device:TPU:0, one launch (start us, length us, event | category | flops | bytes accessed | tf_op | source)
XLA Modules:
  0.0 34.2 jit_solution(2069730347431076241)
XLA Ops:
  0.6 32.2 %shard_map.112 = (bf16[2,4096]{1,0:T(2,128)(2,1)}, bf16[1,40,128]{2,1,0:T(8,128)(2,1)}, bf16[1,40,128]{2,1,0:T(8,128)(2,1)}) custom-call(s32[2]{0:T(128)} %len_ref.1, s32[4]{0:T(128)} %owner_ref.1, bf16[40,4096]{1,0:T(8,128)(2,1)} %stored_ref.1, bf16[2,4096]{1,0:T(2,128)(2,1)} %new_ref.1, bf16[4096,2048]{1,0:T(8,128)(2,1)} %wq_ref.1, ...), custom_call_target="tpu_custom_call" | custom-call | tf_op jit(solution)/shard_map/pallas_call | solution.py:359
  32.8 1.4 %shard_map.113 = (bf16[2,4096]{1,0:T(2,128)(2,1)}, bf16[1,40,128]{2,1,0:T(8,128)(2,1)}, bf16[1,40,128]{2,1,0:T(8,128)(2,1)}) custom-call(bf16[2,4096]{1,0:T(2,128)(2,1)} %get-tuple-element.6.refs_0_, bf16[1,40,128]{2,1,0:T(8,128)(2,1)} %get-tuple-element.7.refs_1_, bf16[1,40,128]{2,1,0:T(8,128)(2,1)} %get-tuple-element.8.refs_2_), custom_call_target="tpu_custom_call" | custom-call | tf_op jit(solution)/shard_map/pallas_call | solution.py:390
